TPU v7x, 32 devices: a whole 2x2x4 slice. The times are simulated.
32 devices in a mesh: dp: 8 (over z, x), seq: 4 (over y, core).
Axes of the slice: x: 2, y: 2, z: 4, core: 2. Of those that a mesh axis runs over, the one named last changes fastest.
Arguments:
- queries: bfloat16 [8, 512, 2048], P('dp', 'seq'), may hold values from -72 to 72
- hit_keys: bfloat16 [8, 512, 2048], P('dp', 'seq'), may hold values from -12 to 12
- hit_values: bfloat16 [8, 512, 2048], P('dp', 'seq'), may hold values from -6 to 6
- hit_counts: int32 [8], P('dp'), may hold values from 128 to 512, as said below
- master_weight: float32 [8, 256, 2048], P('dp', None, 'seq'), may hold values from -0.5 to 0.5
- first_moment: float32 [8, 256, 2048], P('dp', None, 'seq'), may hold values from -4 to 4
- second_moment: float32 [8, 256, 2048], P('dp', None, 'seq'), may hold values from 0.1 to 4
- gradient: float32 [8, 256, 2048], P('dp', None, 'seq'), may hold values from -6 to 6
- owner_bucket: int32 [8], replicated, may hold values from 0 to 7, each once
Outputs:
- projected: bfloat16 [8, 512, 2048], P('dp', 'seq')
- new_master: float32 [8, 256, 2048], P('dp', None, 'seq')
- new_first: float32 [8, 256, 2048], P('dp', None, 'seq')
- new_second: float32 [8, 256, 2048], P('dp', None, 'seq')
Inputs may be any that keep to these rules, and one draw needn't show every extreme that they name: The valid hits of event e are its first hit_counts[e] slots; some event is full. `owner_bucket`: each bucket is held by exactly one owner.
All inputs are finite; a program needn't handle non-finite values.
Results may differ from a plain program's by a relative error of at most 0.0063.
Values may be sent and summed in bfloat16 or wider, within the bound.
No kernel may reach another device: no remote copies, remote signals or barrier semaphores. Data moves between devices by JAX's collectives and lax.ppermute only.
A program may use at most 64 MiB of HBM per device.

v0:
```python
import jax
import jax.numpy as jnp
from jax import lax
from jax.sharding import PartitionSpec as P

HEAD_DIM = 128
beta_one = 0.9
beta_two = 0.999
learn_rate = 0.003
weight_decay = 0.1
epsilon = 1e-08
step_count = 10.0
block_rows = 512


def adam_update(master_weight, first_moment, second_moment, gradient):
    new_first = beta_one * first_moment + (1.0 - beta_one) * gradient
    new_second = beta_two * second_moment + (1.0 - beta_two) * gradient * gradient
    first_hat = new_first / (1.0 - beta_one**step_count)
    second_hat = new_second / (1.0 - beta_two**step_count)
    new_master = master_weight - learn_rate * (
        first_hat / (jnp.sqrt(second_hat) + epsilon) + weight_decay * master_weight
    )
    return (new_master, new_first, new_second)


def attend_head(head_query, head_keys, head_values, count):
    length = head_query.shape[0]
    block = min(block_rows, length)
    scale = head_query.shape[1] ** (-0.5)
    valid = lax.broadcasted_iota(jnp.int32, (1, length), 1) < count

    def one_block(rows):
        scores = (
            lax.dot_general(
                rows, head_keys, (((1,), (1,)), ((), ())), preferred_element_type=jnp.float32
            )
            * scale
        )
        scores = jnp.where(valid, scores, -jnp.inf)
        top = jnp.max(scores, axis=1, keepdims=True)
        expo = jnp.exp(scores - top)
        weights = (expo / jnp.sum(expo, axis=1, keepdims=True)).astype(jnp.bfloat16)
        return jnp.dot(weights, head_values, preferred_element_type=jnp.float32).astype(
            jnp.bfloat16
        )

    blocks = head_query.reshape(length // block, block, head_query.shape[1])
    return lax.map(one_block, blocks).reshape(length, head_query.shape[1])


def body(
    queries,
    hit_keys,
    hit_values,
    hit_counts,
    master_weight,
    first_moment,
    second_moment,
    gradient,
    owner_bucket,
):
    new_master, new_first, new_second = adam_update(
        master_weight, first_moment, second_moment, gradient
    )
    weight_half = new_master.astype(jnp.bfloat16)
    groups = lax.axis_size("seq")
    owners = lax.axis_size("dp")
    tok_rows = queries.shape[1]
    width = queries.shape[2]
    per_group = width // groups
    heads_here = per_group // HEAD_DIM
    count = hit_counts[0]
    matches = owner_bucket[:, None] == jnp.arange(owners, dtype=jnp.int32)[None, :]
    inverse = jnp.sum(jnp.where(matches, jnp.arange(owners, dtype=jnp.int32)[:, None], 0), axis=0)

    def split_heads(array):
        return array.reshape(1, tok_rows, groups, heads_here, HEAD_DIM)

    query_part = lax.all_to_all(
        split_heads(queries), "seq", split_axis=2, concat_axis=1, tiled=True
    )
    keys_part = lax.all_to_all(
        split_heads(hit_keys), "seq", split_axis=2, concat_axis=1, tiled=True
    )
    values_part = lax.all_to_all(
        split_heads(hit_values), "seq", split_axis=2, concat_axis=1, tiled=True
    )
    n_heads = query_part.shape[3]

    def one_head(index):
        head_query = lax.dynamic_index_in_dim(query_part, index, 3, keepdims=False)[0, :, 0, :]
        head_keys = lax.dynamic_index_in_dim(keys_part, index, 3, keepdims=False)[0, :, 0, :]
        head_values = lax.dynamic_index_in_dim(values_part, index, 3, keepdims=False)[0, :, 0, :]
        return attend_head(head_query, head_keys, head_values, count)

    outputs = lax.map(one_head, jnp.arange(n_heads, dtype=jnp.int32))
    attended = jnp.moveaxis(outputs, 0, 1)[None, :, None, :, :]
    returned = lax.all_to_all(attended, "seq", split_axis=1, concat_axis=2, tiled=True)
    rows_in = returned.reshape(tok_rows, width)
    owned = lax.all_gather(weight_half, "dp", axis=0, tiled=True)
    full = lax.all_gather(owned, "seq", axis=2, tiled=True)
    projection = jnp.take(full, inverse, axis=0).reshape(width, width)
    total = jnp.dot(rows_in, projection, preferred_element_type=jnp.float32)
    projected = total.astype(jnp.bfloat16)[None]
    return (projected, new_master, new_first, new_second)


def solution(mesh):
    return jax.shard_map(
        body,
        mesh=mesh,
        in_specs=(
            P("dp", "seq", None),
            P("dp", "seq", None),
            P("dp", "seq", None),
            P("dp"),
            P("dp", None, "seq"),
            P("dp", None, "seq"),
            P("dp", None, "seq"),
            P("dp", None, "seq"),
            P(),
        ),
        out_specs=(
            P("dp", "seq", None),
            P("dp", None, "seq"),
            P("dp", None, "seq"),
            P("dp", None, "seq"),
        ),
        check_vma=False,
    )
```

profile of v0, /device:TPU:0, one launch (start us, length us, event | category | flops | bytes accessed | tf_op | source)
XLA Modules:
  0.0 175.6 jit_solution(9775890406966182870)
XLA Ops:
  7.2 0.0 all-gather.3.cloned.1.call-start
  7.2 3.1 %fusion.15 = (bf16[1,256,512]{2,1,0:T(8,128)(2,1)}, f32[1,256,512]{2,1,0:T(8,128)}, f32[1,256,512]{2,1,0:T(8,128)}, f32[1,256,512]{2,1,0:T(8,128)}) fusion(f32[1,256,512]{2,1,0:T(8,128)} %param.15, f32[1,256,512]{2,1,0:T(8,128)} %param.18, f32[1,256,512]{2,1,0:T(8,128)} %param.16, f32[1,256,512]{2,1,0:T(8,128)} %param.17), kind=kLoop, calls=%fused_computation.33 | loop fusion | flops 2097152 | bytes 3932160 | tf_op jit(solution)/shard_map/convert_element_type | solution.py:66
  10.3 0.0 all-gather.3.cloned.1.call-update
  10.4 0.0 all-gather.5.cloned.1.call-start
  10.4 52.3 %all-gather.3.cloned.1.call-done = bf16[8,256,512]{2,1,0:T(8,128)(2,1)} async-done(((bf16[1,256,512]{2,1,0:T(8,128)(2,1)}), bf16[8,256,512]{2,1,0:T(8,128)(2,1)}) %all-gather.3.cloned.1.call-update) | async-done | bytes 2097168 | tf_op jit(solution)/shard_map/all_gather | solution.py:101
  62.8 1.3 copy.41
  64.1 1.0 copy.42
  65.1 3.5 %all-to-all-start.1 = ((bf16[1,128,4,4,128]{4,1,3,0,2:T(8,128)(2,1)}), bf16[1,128,4,4,128]{4,1,3,0,2:T(8,128)(2,1)S(1)}, u32[]{:S(2)}, u32[]{:S(2)}) async-start(bf16[1,128,4,4,128]{4,1,3,0,2:T(8,128)(2,1)} %copy.42), calls=%async_computation.1 | async-start | bytes 1048576 | tf_op jit(solution)/shard_map/all_to_all | solution.py:83
  68.6 0.3 copy.44
  68.9 1.0 copy.45
  69.9 10.8 %all-to-all-done.1 = bf16[1,128,4,4,128]{4,1,3,0,2:T(8,128)(2,1)S(1)} async-done(((bf16[1,128,4,4,128]{4,1,3,0,2:T(8,128)(2,1)}), bf16[1,128,4,4,128]{4,1,3,0,2:T(8,128)(2,1)S(1)}, u32[]{:S(2)}, u32[]{:S(2)}) %all-to-all-start.1) | async-done | bytes 524320 | tf_op jit(solution)/shard_map/all_to_all | solution.py:83
  80.7 3.5 %all-to-all-start.2 = ((bf16[1,128,4,4,128]{4,1,3,0,2:T(8,128)(2,1)}), bf16[1,128,4,4,128]{4,1,3,0,2:T(8,128)(2,1)S(1)}, u32[]{:S(2)}, u32[]{:S(2)}) async-start(bf16[1,128,4,4,128]{4,1,3,0,2:T(8,128)(2,1)} %copy.45), calls=%async_computation.2 | async-start | bytes 1048576 | tf_op jit(solution)/shard_map/all_to_all | solution.py:86
  84.2 0.3 copy.38
  84.5 1.0 copy.39
  85.5 13.4 %all-to-all-done.2 = bf16[1,128,4,4,128]{4,1,3,0,2:T(8,128)(2,1)S(1)} async-done(((bf16[1,128,4,4,128]{4,1,3,0,2:T(8,128)(2,1)}), bf16[1,128,4,4,128]{4,1,3,0,2:T(8,128)(2,1)S(1)}, u32[]{:S(2)}, u32[]{:S(2)}) %all-to-all-start.2) | async-done | bytes 524320 | tf_op jit(solution)/shard_map/all_to_all | solution.py:86
  99.0 3.5 %all-to-all-start = ((bf16[1,128,4,4,128]{4,1,3,0,2:T(8,128)(2,1)}), bf16[1,128,4,4,128]{4,1,3,0,2:T(8,128)(2,1)S(1)}, u32[]{:S(2)}, u32[]{:S(2)}) async-start(bf16[1,128,4,4,128]{4,1,3,0,2:T(8,128)(2,1)} %copy.39), calls=%async_computation | async-start | bytes 1048576 | tf_op jit(solution)/shard_map/all_to_all | solution.py:80
  102.5 0.1 select_reduce_fusion
  102.6 14.5 %all-to-all-done = bf16[1,128,4,4,128]{4,1,3,0,2:T(8,128)(2,1)S(1)} async-done(((bf16[1,128,4,4,128]{4,1,3,0,2:T(8,128)(2,1)}), bf16[1,128,4,4,128]{4,1,3,0,2:T(8,128)(2,1)S(1)}, u32[]{:S(2)}, u32[]{:S(2)}) %all-to-all-start) | async-done | bytes 524320 | tf_op jit(solution)/shard_map/all_to_all | solution.py:80
  117.2 16.6 %while.10 = (s32[]{:T(128)}, bf16[4,512,128]{2,1,0:T(8,128)(2,1)S(1)}, s32[]{:T(128)}, s32[4]{0:T(128)S(1)}, bf16[1,512,1,4,128]{4,1,3,2,0:T(8,128)(2,1)S(1)}, /...) while((s32[]{:T(128)}, ...), condition=%wide.region_3.4_spmd, body=%wide.region_0.3_spmd.sunk | while | flops 136379904 | bytes 3682463 | solution.py:97
  117.3 0.6 dynamic_slice.40
  119.8 0.7 iota_compare_fusion.3
  120.4 0.3 fusion.25
  120.8 0.2 fusion.26
  121.0 0.4 fusion.27
  121.4 0.6 dynamic_slice.40
  123.9 0.7 iota_compare_fusion.3
  124.6 0.3 fusion.25
  124.9 0.2 fusion.26
  125.1 0.4 fusion.27
  125.6 0.6 dynamic_slice.40
  128.1 0.7 iota_compare_fusion.3
  128.8 0.3 fusion.25
  129.1 0.2 fusion.26
  129.3 0.4 fusion.27
  129.7 0.6 dynamic_slice.40
  132.3 0.7 iota_compare_fusion.3
  132.9 0.3 fusion.25
  133.2 0.2 fusion.26
  133.4 0.4 fusion.27
  133.9 1.2 copy.51
  135.1 3.5 %all-to-all-start.3 = ((bf16[1,512,1,4,128]{4,3,2,0,1:T(4,128)(2,1)}), bf16[1,512,1,4,128]{4,3,2,0,1:T(4,128)(2,1)S(1)}, u32[]{:S(2)}, u32[]{:S(2)}) async-start(bf16[1,512,1,4,128]{4,3,2,0,1:T(4,128)(2,1)} %bitcast.54), calls=%async_computation.3 | async-start | bytes 1048576 | tf_op jit(solution)/shard_map/all_to_all | solution.py:99
  138.6 8.8 %all-to-all-done.3 = bf16[1,512,1,4,128]{4,3,2,0,1:T(4,128)(2,1)S(1)} async-done(((bf16[1,512,1,4,128]{4,3,2,0,1:T(4,128)(2,1)}), bf16[1,512,1,4,128]{4,3,2,0,1:T(4,128)(2,1)S(1)}, u32[]{:S(2)}, u32[]{:S(2)}) %all-to-all-start.3) | async-done | bytes 524320 | tf_op jit(solution)/shard_map/all_to_all | solution.py:99
  147.4 0.1 copy.48
  147.4 0.3 copy.49
  147.7 0.0 all-gather.5.cloned.1.call-done
  147.8 8.1 %gather_fusion = bf16[8,256,2048]{2,1,0:T(8,128)(2,1)} fusion(bf16[8,256,2048]{2,1,0:T(8,128)(2,1)} %all-gather.5.cloned.1.call-done, s32[1024]{0:T(1024)S(1)} %pad_clamp_fusion), kind=kCustom, calls=%fused_computation | custom fusion | bytes 16777248 | tf_op jit(solution)/shard_map/jit(_take)/gather | solution.py:103
  155.8 7.5 %broadcast_select_fusion = bf16[8,256,2048]{2,1,0:T(8,128)(2,1)} fusion(bf16[8,256,2048]{2,1,0:T(8,128)(2,1)} %gather_fusion, pred[8]{0:T(512)(128)(4,1)S(1)} %compare_and_fusion), kind=kLoop, calls=%fused_computation.18 | loop fusion | flops 4194304 | bytes 16777224 | tf_op jit(solution)/shard_map/jit(_take)/select_n | solution.py:103
  163.3 5.5 %fusion.12 = bf16[1,128,2048]{2,1,0:T(8,128)(2,1)} fusion(bf16[128,2048]{0,1:T(8,128)(2,1)S(1)} %bitcast.66, bf16[2048,2048]{1,0:T(8,128)(2,1)} %bitcast.65), kind=kOutput, calls=%fused_computation.20 | convolution fusion | flops 1074003968 | bytes 9437184 | tf_op jit(solution)/shard_map/dot_general | solution.py:104
  (15 shorter events, 0.2 us)
Async XLA Ops:
  7.2 61.4 %copy-start = (bf16[1,128,2048]{2,1,0:T(8,128)(2,1)S(1)}, bf16[1,128,2048]{2,1,0:T(8,128)(2,1)}, u32[]{:S(2)}) copy-start(bf16[1,128,2048]{2,1,0:T(8,128)(2,1)} %param.13) | copy-start | bytes 1572868
  7.2 77.0 %copy-start.1 = (bf16[1,128,2048]{2,1,0:T(8,128)(2,1)S(1)}, bf16[1,128,2048]{2,1,0:T(8,128)(2,1)}, u32[]{:S(2)}) copy-start(bf16[1,128,2048]{2,1,0:T(8,128)(2,1)} %param.11) | copy-start | bytes 1572868
  7.2 95.3 %copy-start.2 = (s32[8]{0:T(128)S(1)}, s32[8]{0:T(128)}, u32[]{:S(2)}) copy-start(s32[8]{0:T(128)} %param.19) | copy-start | bytes 100
  7.2 55.6 %all-gather.3.cloned.1.call-start = ((), (), s32[]{:S(2)}) async-start(), calls=%async_computation.4 | async-start | bytes 2359296 | tf_op jit(solution)/shard_map/all_gather | solution.py:101
  10.4 137.4 %all-gather.5.cloned.1.call-start = ((), (), s32[]{:S(2)}) async-start(), calls=%async_computation.5 | async-start | bytes 10485760 | tf_op jit(solution)/shard_map/all_gather | solution.py:102
  65.1 15.6 %all-to-all-start.1 = ((bf16[1,128,4,4,128]{4,1,3,0,2:T(8,128)(2,1)}), bf16[1,128,4,4,128]{4,1,3,0,2:T(8,128)(2,1)S(1)}, u32[]{:S(2)}, u32[]{:S(2)}) async-start(bf16[1,128,4,4,128]{4,1,3,0,2:T(8,128)(2,1)} %copy.42), calls=%async_computation.1 | async-start | bytes 1048576 | tf_op jit(solution)/shard_map/all_to_all | solution.py:83
  80.7 18.2 %all-to-all-start.2 = ((bf16[1,128,4,4,128]{4,1,3,0,2:T(8,128)(2,1)}), bf16[1,128,4,4,128]{4,1,3,0,2:T(8,128)(2,1)S(1)}, u32[]{:S(2)}, u32[]{:S(2)}) async-start(bf16[1,128,4,4,128]{4,1,3,0,2:T(8,128)(2,1)} %copy.45), calls=%async_computation.2 | async-start | bytes 1048576 | tf_op jit(solution)/shard_map/all_to_all | solution.py:86
  99.0 18.2 %all-to-all-start = ((bf16[1,128,4,4,128]{4,1,3,0,2:T(8,128)(2,1)}), bf16[1,128,4,4,128]{4,1,3,0,2:T(8,128)(2,1)S(1)}, u32[]{:S(2)}, u32[]{:S(2)}) async-start(bf16[1,128,4,4,128]{4,1,3,0,2:T(8,128)(2,1)} %copy.39), calls=%async_computation | async-start | bytes 1048576 | tf_op jit(solution)/shard_map/all_to_all | solution.py:80
  135.1 12.3 %all-to-all-start.3 = ((bf16[1,512,1,4,128]{4,3,2,0,1:T(4,128)(2,1)}), bf16[1,512,1,4,128]{4,3,2,0,1:T(4,128)(2,1)S(1)}, u32[]{:S(2)}, u32[]{:S(2)}) async-start(bf16[1,512,1,4,128]{4,3,2,0,1:T(4,128)(2,1)} %bitcast.54), calls=%async_computation.3 | async-start | bytes 1048576 | tf_op jit(solution)/shard_map/all_to_all | solution.py:99
Sparse Core Ops, SparseCore 0:
  10.7 51.9 all-gather.2
  64.3 71.0 all-gather.4
where the time goes:
time: 176 us
  waiting for transfers between devices  100 us (57%)
  local copies, waits for them, and re-layouts  17 us (10%)
  between operations  14.2 us (8%)
  other arithmetic  14.1 us (8%)
  starting transfers between devices  14 us (8%)
  matrix products  8.47 us (5%)
  loops' own time  7.88 us (4%)
    all_gather x1, waiting for transfers between devices, body(): owned = lax.all_gather(weight_half, 'dp', axis=0, tiled=True)  52.3 us
    all_to_all x1, waiting for transfers between devices, body(): lax.all_to_all(split_heads(queries), 'seq', split_axis=2, concat_axis=1,...  14.5 us
    all_to_all x1, waiting for transfers between devices, body(): lax.all_to_all(split_heads(hit_values), 'seq', split_axis=2, concat_axis=...  13.4 us
    all_to_all x1, waiting for transfers between devices, body(): lax.all_to_all(split_heads(hit_keys), 'seq', split_axis=2, concat_axis=1,...  10.8 us
    all_to_all x1, waiting for transfers between devices, body(): lax.all_to_all(attended, 'seq', split_axis=1, concat_axis=2, tiled=True)  8.77 us
    gather x1, local copies, waits for them, and re-layouts, body(): projection = jnp.take(full, inverse, axis=0).reshape(width, width)  8.08 us
    another operation x1, loops' own time, body(): outputs = lax.map(one_head, jnp.arange(n_heads, dtype=jnp.int32))  7.88 us
    select_n x2, other arithmetic, body(): projection = jnp.take(full, inverse, axis=0).reshape(width, width)  7.49 us
  transfers between devices with their start and end apart: 6, of which 5 were waited for; matrix products, arithmetic and copies ran while one was open for 9% of the time, Pallas kernels for 0%

commit v1 on v0

--- a/solution.py
+++ b/solution.py
@@ -96,7 +96,10 @@
 
     outputs = lax.map(one_head, jnp.arange(n_heads, dtype=jnp.int32))
     attended = jnp.moveaxis(outputs, 0, 1)[None, :, None, :, :]
-    returned = lax.all_to_all(attended, "seq", split_axis=1, concat_axis=2, tiled=True)
+    returned = jnp.concatenate(
+        lax.all_to_all(jnp.stack(jnp.split(attended, lax.axis_size("seq"), axis=1)), "seq", 0, 0),
+        axis=2,
+    )
     rows_in = returned.reshape(tok_rows, width)
     owned = lax.all_gather(weight_half, "dp", axis=0, tiled=True)
     full = lax.all_gather(owned, "seq", axis=2, tiled=True)

time: 176 us -> 167 us (0.949)
  waiting for transfers between devices: 100 us -> 91.2 us
    all_to_all x1, waiting for transfers between devices: 8.77 us -> 0.01 us  [body(): lax.all_to_all(jnp.stack(jnp.split(attended, lax.axis_size('seq'), axis=1...]
    all_to_all x1, waiting for transfers between devices: 14.5 us -> 10.8 us  [body(): lax.all_to_all(split_heads(queries), 'seq', split_axis=2, concat_axis=1,...]
    all_to_all x1, waiting for transfers between devices: 10.8 us -> 13.4 us  [body(): lax.all_to_all(split_heads(hit_keys), 'seq', split_axis=2, concat_axis=1,...]
  transfers between devices with their start and end apart: 6 -> 6, of which waited for: 5 -> 4; matrix products, arithmetic and copies ran while one was open for 9% -> 18% of each run, Pallas kernels for 0% -> 0%
where the time goes in v1:
time: 167 us
  waiting for transfers between devices  91.2 us (55%)
  local copies, waits for them, and re-layouts  16.1 us (10%)
  other arithmetic  14.9 us (9%)
  between operations  14.2 us (9%)
  starting transfers between devices  14 us (8%)
  matrix products  8.24 us (5%)
  loops' own time  7.97 us (5%)
    all_gather x1, waiting for transfers between devices, body(): owned = lax.all_gather(weight_half, 'dp', axis=0, tiled=True)  52.3 us
    all_to_all x1, waiting for transfers between devices, body(): lax.all_to_all(split_heads(hit_values), 'seq', split_axis=2, concat_axis=...  14.6 us
    all_to_all x1, waiting for transfers between devices, body(): lax.all_to_all(split_heads(hit_keys), 'seq', split_axis=2, concat_axis=1,...  13.4 us
    all_to_all x1, waiting for transfers between devices, body(): lax.all_to_all(split_heads(queries), 'seq', split_axis=2, concat_axis=1,...  10.8 us
    gather x1, local copies, waits for them, and re-layouts, body(): projection = jnp.take(full, inverse, axis=0).reshape(width, width)  8.07 us
    another operation x1, loops' own time, body(): outputs = lax.map(one_head, jnp.arange(n_heads, dtype=jnp.int32))  7.97 us
    select_n x2, other arithmetic, body(): projection = jnp.take(full, inverse, axis=0).reshape(width, width)  7.48 us
    dot_general x1, matrix products, body(): total = jnp.dot(rows_in, projection, preferred_element_type=jnp.float32)  5.46 us
  transfers between devices with their start and end apart: 6, of which 4 were waited for; matrix products, arithmetic and copies ran while one was open for 18% of the time, Pallas kernels for 0%

profile of v1, /device:TPU:0, one launch (start us, length us, event | category | flops | bytes accessed | tf_op | source)
XLA Modules:
  0.0 166.6 jit_solution(13997543822994115507)
XLA Ops:
  7.2 0.0 all-gather.3.cloned.1.call-start
  7.2 3.1 %fusion.14 = (bf16[1,256,512]{2,1,0:T(8,128)(2,1)}, f32[1,256,512]{2,1,0:T(8,128)}, f32[1,256,512]{2,1,0:T(8,128)}, f32[1,256,512]{2,1,0:T(8,128)}) fusion(f32[1,256,512]{2,1,0:T(8,128)} %param.15, f32[1,256,512]{2,1,0:T(8,128)} %param.18, f32[1,256,512]{2,1,0:T(8,128)} %param.16, f32[1,256,512]{2,1,0:T(8,128)} %param.17), kind=kLoop, calls=%fused_computation.37 | loop fusion | flops 2097152 | bytes 3932160 | tf_op jit(solution)/shard_map/convert_element_type | solution.py:66
  10.4 0.0 all-gather.5.cloned.1.call-start
  10.4 52.3 %all-gather.3.cloned.1.call-done = bf16[8,256,512]{2,1,0:T(8,128)(2,1)} async-done(((bf16[1,256,512]{2,1,0:T(8,128)(2,1)}), bf16[8,256,512]{2,1,0:T(8,128)(2,1)}) %all-gather.3.cloned.1.call-update) | async-done | bytes 2097168 | tf_op jit(solution)/shard_map/all_gather | solution.py:104
  62.8 1.3 copy.36
  64.1 1.0 copy.37
  65.1 3.5 %all-to-all-start = ((bf16[1,128,4,4,128]{4,1,3,0,2:T(8,128)(2,1)}), bf16[1,128,4,4,128]{4,1,3,0,2:T(8,128)(2,1)S(1)}, u32[]{:S(2)}, u32[]{:S(2)}) async-start(bf16[1,128,4,4,128]{4,1,3,0,2:T(8,128)(2,1)} %copy.37), calls=%async_computation | async-start | bytes 1048576 | tf_op jit(solution)/shard_map/all_to_all | solution.py:80
  68.6 0.3 copy.39
  68.9 1.0 copy.40
  69.9 10.8 %all-to-all-done = bf16[1,128,4,4,128]{4,1,3,0,2:T(8,128)(2,1)S(1)} async-done(((bf16[1,128,4,4,128]{4,1,3,0,2:T(8,128)(2,1)}), bf16[1,128,4,4,128]{4,1,3,0,2:T(8,128)(2,1)S(1)}, u32[]{:S(2)}, u32[]{:S(2)}) %all-to-all-start) | async-done | bytes 524320 | tf_op jit(solution)/shard_map/all_to_all | solution.py:80
  80.7 3.5 %all-to-all-start.1 = ((bf16[1,128,4,4,128]{4,1,3,0,2:T(8,128)(2,1)}), bf16[1,128,4,4,128]{4,1,3,0,2:T(8,128)(2,1)S(1)}, u32[]{:S(2)}, u32[]{:S(2)}) async-start(bf16[1,128,4,4,128]{4,1,3,0,2:T(8,128)(2,1)} %copy.40), calls=%async_computation.1 | async-start | bytes 1048576 | tf_op jit(solution)/shard_map/all_to_all | solution.py:83
  84.2 0.3 copy.42
  84.5 1.0 copy.43
  85.5 0.1 select_reduce_fusion
  85.6 13.4 %all-to-all-done.1 = bf16[1,128,4,4,128]{4,1,3,0,2:T(8,128)(2,1)S(1)} async-done(((bf16[1,128,4,4,128]{4,1,3,0,2:T(8,128)(2,1)}), bf16[1,128,4,4,128]{4,1,3,0,2:T(8,128)(2,1)S(1)}, u32[]{:S(2)}, u32[]{:S(2)}) %all-to-all-start.1) | async-done | bytes 524320 | tf_op jit(solution)/shard_map/all_to_all | solution.py:83
  99.0 3.5 %all-to-all-start.2 = ((bf16[1,128,4,4,128]{4,1,3,0,2:T(8,128)(2,1)}), bf16[1,128,4,4,128]{4,1,3,0,2:T(8,128)(2,1)S(1)}, u32[]{:S(2)}, u32[]{:S(2)}) async-start(bf16[1,128,4,4,128]{4,1,3,0,2:T(8,128)(2,1)} %copy.43), calls=%async_computation.2 | async-start | bytes 1048576 | tf_op jit(solution)/shard_map/all_to_all | solution.py:86
  102.6 14.6 %all-to-all-done.2 = bf16[1,128,4,4,128]{4,1,3,0,2:T(8,128)(2,1)S(1)} async-done(((bf16[1,128,4,4,128]{4,1,3,0,2:T(8,128)(2,1)}), bf16[1,128,4,4,128]{4,1,3,0,2:T(8,128)(2,1)S(1)}, u32[]{:S(2)}, u32[]{:S(2)}) %all-to-all-start.2) | async-done | bytes 524320 | tf_op jit(solution)/shard_map/all_to_all | solution.py:86
  117.2 17.0 %while.10 = (s32[]{:T(128)}, bf16[4,512,128]{1,2,0:T(8,128)(2,1)S(1)}, s32[]{:T(128)}, s32[4]{0:T(128)S(1)}, bf16[1,512,1,4,128]{4,1,3,2,0:T(8,128)(2,1)S(1)}, /...) while((s32[]{:T(128)}, ...), condition=%wide.region_3.4_spmd, body=%wide.region_0.3_spmd.sunk | while | flops 136379904 | bytes 4206759 | solution.py:97
  117.3 0.6 dynamic_slice.40
  119.8 0.7 iota_compare_fusion.3
  120.4 0.3 fusion.24
  120.8 0.2 fusion.25
  121.0 0.4 fusion.26
  121.3 0.1 copy.50
  121.5 0.6 dynamic_slice.40
  124.0 0.7 iota_compare_fusion.3
  124.7 0.3 fusion.24
  125.0 0.2 fusion.25
  125.2 0.4 fusion.26
  125.6 0.1 copy.50
  125.8 0.6 dynamic_slice.40
  128.3 0.7 iota_compare_fusion.3
  129.0 0.3 fusion.24
  129.3 0.2 fusion.25
  129.5 0.4 fusion.26
  129.9 0.1 copy.50
  130.0 0.6 dynamic_slice.40
  132.5 0.7 iota_compare_fusion.3
  133.2 0.3 fusion.24
  133.5 0.2 fusion.25
  133.7 0.4 fusion.26
  134.1 0.1 copy.50
  134.3 0.1 slice_bitcast_fusion.3
  134.4 0.9 pad_maximum_fusion
  135.3 3.5 %all-to-all-start.3 = ((bf16[4,1,128,1,4,128]{2,5,4,3,1,0:T(8,128)(2,1)}), bf16[4,1,128,1,4,128]{2,5,4,3,1,0:T(8,128)(2,1)S(1)}, u32[]{:S(2)}, u32[]{:S(2)}) async-start(bf16[4,1,128,1,4,128]{2,5,4,3,1,0:T(8,128)(2,1)} %pad_maximum_fusion), calls=%async_computation.3 | async-start | bytes 1048576 | tf_op jit(solution)/shard_map/all_to_all | solution.py:100
  138.8 8.1 %gather_fusion = bf16[8,256,2048]{2,1,0:T(8,128)(2,1)} fusion(bf16[8,256,2048]{2,1,0:T(8,128)(2,1)} %all-gather.5.cloned.1.call-done, s32[1024]{0:T(1024)S(1)} %pad_clamp_fusion), kind=kCustom, calls=%fused_computation | custom fusion | bytes 16777248 | tf_op jit(solution)/shard_map/jit(_take)/gather | solution.py:106
  146.8 7.5 %broadcast_select_fusion = bf16[8,256,2048]{2,1,0:T(8,128)(2,1)} fusion(bf16[8,256,2048]{2,1,0:T(8,128)(2,1)} %gather_fusion, pred[8]{0:T(512)(128)(4,1)S(1)} %compare_and_fusion), kind=kLoop, calls=%fused_computation.18 | loop fusion | flops 4194304 | bytes 16777224 | tf_op jit(solution)/shard_map/jit(_take)/select_n | solution.py:106
  154.3 5.5 %fusion.11 = bf16[1,128,2048]{2,1,0:T(8,128)(2,1)} fusion(bf16[128,2048]{0,1:T(8,128)(2,1)S(1)} %bitcast.71, bf16[2048,2048]{1,0:T(8,128)(2,1)} %bitcast.70), kind=kOutput, calls=%fused_computation.20 | convolution fusion | flops 1074003968 | bytes 9437184 | tf_op jit(solution)/shard_map/dot_general | solution.py:107
  (22 shorter events, 0.3 us)
Async XLA Ops:
  7.2 61.4 %copy-start = (bf16[1,128,2048]{2,1,0:T(8,128)(2,1)S(1)}, bf16[1,128,2048]{2,1,0:T(8,128)(2,1)}, u32[]{:S(2)}) copy-start(bf16[1,128,2048]{2,1,0:T(8,128)(2,1)} %param.12) | copy-start | bytes 1572868
  7.2 77.0 %copy-start.1 = (bf16[1,128,2048]{2,1,0:T(8,128)(2,1)S(1)}, bf16[1,128,2048]{2,1,0:T(8,128)(2,1)}, u32[]{:S(2)}) copy-start(bf16[1,128,2048]{2,1,0:T(8,128)(2,1)} %param.13) | copy-start | bytes 1572868
  7.2 78.3 %copy-start.2 = (s32[8]{0:T(128)S(1)}, s32[8]{0:T(128)}, u32[]{:S(2)}) copy-start(s32[8]{0:T(128)} %param.19) | copy-start | bytes 100
  7.2 55.6 %all-gather.3.cloned.1.call-start = ((), (), s32[]{:S(2)}) async-start(), calls=%async_computation.4 | async-start | bytes 2359296 | tf_op jit(solution)/shard_map/all_gather | solution.py:104
  10.4 128.4 %all-gather.5.cloned.1.call-start = ((), (), s32[]{:S(2)}) async-start(), calls=%async_computation.5 | async-start | bytes 10485760 | tf_op jit(solution)/shard_map/all_gather | solution.py:105
  65.1 15.6 %all-to-all-start = ((bf16[1,128,4,4,128]{4,1,3,0,2:T(8,128)(2,1)}), bf16[1,128,4,4,128]{4,1,3,0,2:T(8,128)(2,1)S(1)}, u32[]{:S(2)}, u32[]{:S(2)}) async-start(bf16[1,128,4,4,128]{4,1,3,0,2:T(8,128)(2,1)} %copy.37), calls=%async_computation | async-start | bytes 1048576 | tf_op jit(solution)/shard_map/all_to_all | solution.py:80
  80.7 18.2 %all-to-all-start.1 = ((bf16[1,128,4,4,128]{4,1,3,0,2:T(8,128)(2,1)}), bf16[1,128,4,4,128]{4,1,3,0,2:T(8,128)(2,1)S(1)}, u32[]{:S(2)}, u32[]{:S(2)}) async-start(bf16[1,128,4,4,128]{4,1,3,0,2:T(8,128)(2,1)} %copy.40), calls=%async_computation.1 | async-start | bytes 1048576 | tf_op jit(solution)/shard_map/all_to_all | solution.py:83
  99.0 18.2 %all-to-all-start.2 = ((bf16[1,128,4,4,128]{4,1,3,0,2:T(8,128)(2,1)}), bf16[1,128,4,4,128]{4,1,3,0,2:T(8,128)(2,1)S(1)}, u32[]{:S(2)}, u32[]{:S(2)}) async-start(bf16[1,128,4,4,128]{4,1,3,0,2:T(8,128)(2,1)} %copy.43), calls=%async_computation.2 | async-start | bytes 1048576 | tf_op jit(solution)/shard_map/all_to_all | solution.py:86
  135.3 19.1 %all-to-all-start.3 = ((bf16[4,1,128,1,4,128]{2,5,4,3,1,0:T(8,128)(2,1)}), bf16[4,1,128,1,4,128]{2,5,4,3,1,0:T(8,128)(2,1)S(1)}, u32[]{:S(2)}, u32[]{:S(2)}) async-start(bf16[4,1,128,1,4,128]{2,5,4,3,1,0:T(8,128)(2,1)} %pad_maximum_fusion), calls=%async_computation.3 | async-start | bytes 1048576 | tf_op jit(solution)/shard_map/all_to_all | solution.py:100
Sparse Core Ops, SparseCore 0:
  10.7 51.9 all-gather.2
  64.3 71.0 all-gather.4
